TPU v7x, 32 devices: a whole 2x2x4 slice. The times are simulated.
32 devices in a mesh: group: 2 (over y), row: 8 (over z, x), col: 2 (over core).
Axes of the slice: x: 2, y: 2, z: 4, core: 2. Of those that a mesh axis runs over, the one named last changes fastest.
Arguments:
- map_in: bfloat16 [192, 96, 48], P(('group', 'row'), 'col'), parts along dimension 0, may hold values from -6 to 6
- embedding: bfloat16 [192, 96], P(('group', 'row')), parts along dimension 0, may hold values from -6 to 6
- w_row: bfloat16 [96, 48], replicated, may hold values from -0.625 to 0.625
- w_col: bfloat16 [96, 48], replicated, may hold values from -0.625 to 0.625
- first_kernel_weight: bfloat16 [3, 3, 48, 48], replicated, may hold values from -0.3125 to 0.3125
- first_bias: float32 [48], replicated, may hold values from -0.5 to 0.5
- second_kernel_weight: bfloat16 [3, 3, 48, 48], replicated, may hold values from -0.3125 to 0.3125
- second_bias: float32 [48], replicated, may hold values from -0.5 to 0.5
- w_mix: bfloat16 [48, 48], replicated, may hold values from -0.875 to 0.875
- b_mix: float32 [48], replicated, may hold values from -0.5 to 0.5
- w_head: float32 [48], replicated, may hold values from -0.875 to 0.875
Outputs:
- contacts: float32 [192, 96], P(('group', 'row'), 'col'), parts along dimension 0
There are 2 independent parts, one for each index of `group`. A program takes and returns all parts, laid end to end along the dimension named above; an argument that names none is the same for every part. Nothing has to cross between parts.
All inputs are finite; a program needn't handle non-finite values.
Results may differ from a plain program's by a relative error of at most 0.0055.
Values may be sent and summed in bfloat16 or wider, within the bound.
A program may use at most 64 MiB of HBM per device.

v0:
```python
import jax
import jax.numpy as jnp
from jax import lax
from jax.sharding import PartitionSpec as P

FIRST_DILATION = 4
SECOND_DILATION = 8


def padded(array, sides, width):
    for axis, dim in sides:
        peers, length = (lax.axis_size(axis), array.shape[dim])
        up = [(i, (i + 1) % peers) for i in range(peers - 1)]
        down = [(j, i) for i, j in up]
        last = lax.slice_in_dim(array, length - width, length, axis=dim)
        leading = lax.slice_in_dim(array, 0, width, axis=dim)
        before = lax.ppermute(last, axis, up)
        after = lax.ppermute(leading, axis, down)
        array = jnp.concatenate([before, array, after], axis=dim)
    return array


def swapped(value, axis, bit):
    mask = 2**bit
    pairs = [(source, source ^ mask) for source in range(lax.axis_size(axis))]
    return lax.ppermute(value, axis, pairs)


def dilated_conv(active, weight, spacing, out_rows, out_cols):
    windows = []
    for tap_row in range(3):
        for tap_col in range(3):
            windows.append(
                active[
                    tap_row * spacing : tap_row * spacing + out_rows,
                    tap_col * spacing : tap_col * spacing + out_cols,
                ]
            )
    stacked = jnp.concatenate(windows, axis=-1)
    flat_weight = weight.reshape(9 * weight.shape[2], weight.shape[3])
    return jnp.einsum("rch,hk->rck", stacked, flat_weight, preferred_element_type=jnp.float32)


def on_device(
    map_in,
    embedding,
    w_row,
    w_col,
    first_kernel_weight,
    first_bias,
    second_kernel_weight,
    second_bias,
    w_mix,
    b_mix,
    w_head,
):
    patch_rows, patch_columns, channels = map_in.shape
    row_count = lax.axis_size("row")
    row_at = lax.axis_index("row")
    col_at = lax.axis_index("col")
    all_bins = lax.all_gather(embedding, "row", axis=0, tiled=True)
    row_terms = jnp.dot(all_bins, w_row, preferred_element_type=jnp.float32)
    col_terms = jnp.dot(all_bins, w_col, preferred_element_type=jnp.float32)
    own_rows = lax.dynamic_slice_in_dim(row_terms, row_at * patch_rows, patch_rows, 0)
    own_cols = lax.dynamic_slice_in_dim(col_terms, col_at * patch_columns, patch_columns, 0)
    contact_grid = (
        map_in.astype(jnp.float32) + own_rows[:, None, :] + own_cols[None, :, :]
    ).astype(jnp.bfloat16)
    first_padded = padded(contact_grid, (("row", 0), ("col", 1)), FIRST_DILATION)
    first_layer = (
        contact_grid.astype(jnp.float32)
        + dilated_conv(
            jnp.maximum(first_padded, 0),
            first_kernel_weight,
            FIRST_DILATION,
            patch_rows,
            patch_columns,
        )
        + first_bias
    ).astype(jnp.bfloat16)
    second_padded = padded(first_layer, (("row", 0), ("col", 1)), SECOND_DILATION)
    second_layer = (
        first_layer.astype(jnp.float32)
        + dilated_conv(
            jnp.maximum(second_padded, 0),
            second_kernel_weight,
            SECOND_DILATION,
            patch_rows,
            patch_columns,
        )
        + second_bias
    ).astype(jnp.bfloat16)
    half_rows = patch_rows // 2
    blocks_per = row_count // 2
    arranged = second_layer.reshape(2, half_rows, blocks_per, patch_rows, channels)
    arranged = arranged.transpose(0, 2, 1, 3, 4).reshape(
        2 * blocks_per, half_rows, patch_rows, channels
    )
    exchanged = lax.all_to_all(
        lax.all_to_all(arranged, "row", split_axis=0, concat_axis=0, tiled=True),
        "col",
        split_axis=0,
        concat_axis=0,
        tiled=True,
    )
    exchanged = exchanged.reshape(2, blocks_per, half_rows, patch_rows, channels)
    top_half = row_at // blocks_per
    kept_part = lax.dynamic_index_in_dim(exchanged, top_half, 0, keepdims=False)
    sent_part = lax.dynamic_index_in_dim(exchanged, 1 - top_half, 0, keepdims=False)
    came_back = swapped(sent_part, "row", blocks_per.bit_length() - 1)
    stacked = jnp.where(
        top_half == 0, jnp.stack([kept_part, came_back]), jnp.stack([came_back, kept_part])
    )
    mirrored = stacked.transpose(3, 1, 0, 2, 4).reshape(patch_rows, patch_columns, channels)
    symmetric = ((second_layer.astype(jnp.float32) + mirrored.astype(jnp.float32)) * 0.5).astype(
        jnp.bfloat16
    )
    mixture = (
        jnp.einsum("rch,hk->rck", symmetric, w_mix, preferred_element_type=jnp.float32) + b_mix
    )
    mixture = jnp.maximum(mixture, 0.0)
    return jnp.sum(mixture * w_head, axis=-1)


def solution(mesh):
    placed = (
        P(("group", "row"), "col", None),
        P(("group", "row"), None),
        P(),
        P(),
        P(),
        P(),
        P(),
        P(),
        P(),
        P(),
        P(),
    )
    return jax.shard_map(
        on_device, mesh=mesh, in_specs=placed, out_specs=P(("group", "row"), "col"), check_vma=False
    )
```

profile of v0, /device:TPU:0, one launch (start us, length us, event | category | flops | bytes accessed | tf_op | source)
XLA Modules:
  0.0 92.6 jit_solution(15328792908924847365)
XLA Ops:
  0.0 0.7 copy-done.5
  0.7 32.3 %all-gather = bf16[8,12,96]{2,1,0:T(8,128)(2,1)S(1)} all-gather(bf16[1,12,96]{2,1,0:T(8,128)(2,1)S(1)} %bitcast.32), channel_id=1, replica_groups=mesh['group'=2,'row'=8,'col'=2] {'row'}, dimensions={0}, use_global_device_ids=true | all-gather | bytes 20736 | tf_op jit(solution)/shard_map/all_gather | solution.py:61
  33.1 0.1 fusion.14
  33.2 0.1 fusion.15
  33.4 0.6 copy-done.1
  34.0 3.4 %collective-permute-start = (bf16[4,48,48]{2,1,0:T(8,128)(2,1)S(1)}, bf16[4,48,48]{2,1,0:T(8,128)(2,1)S(1)}, u32[]{:S(2)}, u32[]{:S(2)}) collective-permute-start(bf16[4,48,48]{2,1,0:T(8,128)(2,1)S(1)} %get-tuple-element.31), channel_id=1, source_target_pairs={{0,2},{2,4},{4,6},{6,8},{8,10},{10,12},{12,14},{1,3},{3,5},{5,7},{... | collective-permute-start | bytes 55304 | tf_op jit(solution)/shard_map/ppermute | solution.py:17
  37.4 1.3 %collective-permute-start.1 = (bf16[4,48,48]{2,1,0:T(8,128)(2,1)S(1)}, bf16[4,48,48]{2,1,0:T(8,128)(2,1)S(1)}, u32[]{:S(2)}, u32[]{:S(2)}) collective-permute-start(bf16[4,48,48]{2,1,0:T(8,128)(2,1)S(1)} %get-tuple-element.32), channel_id=1, source_target_pairs={{2,0},{4,2},{6,4},{8,6},{10,8},{12,10},{14,12},{3,1},{5,3},{7,5},{... | collective-permute-start | bytes 55304 | tf_op jit(solution)/shard_map/ppermute | solution.py:18
  38.7 0.4 collective-permute-done
  39.2 4.3 %collective-permute-done.1 = bf16[4,48,48]{2,1,0:T(8,128)(2,1)S(1)} collective-permute-done((bf16[4,48,48]{2,1,0:T(8,128)(2,1)S(1)}, bf16[4,48,48]{2,1,0:T(8,128)(2,1)S(1)}, u32[]{:S(2)}, u32[]{:S(2)}) %collective-permute-start.1) | collective-permute-done | bytes 18464 | tf_op jit(solution)/shard_map/ppermute | solution.py:18
  43.4 1.3 %collective-permute-start.2 = (bf16[20,4,48]{2,1,0:T(4,128)(2,1)S(1)}, bf16[20,4,48]{2,1,0:T(4,128)(2,1)S(1)}, u32[]{:S(2)}, u32[]{:S(2)}) collective-permute-start(bf16[20,4,48]{2,1,0:T(4,128)(2,1)S(1)} %get-tuple-element.25), channel_id=1, source_target_pairs={{0,1},{2,3},{4,5},{6,7},{8,9},{10,11},{12,13},{14,15},{16,17},{18,... | collective-permute-start | bytes 23048 | tf_op jit(solution)/shard_map/ppermute | solution.py:17
  44.7 1.3 %collective-permute-start.3 = (bf16[20,4,48]{2,1,0:T(4,128)(2,1)S(1)}, bf16[20,4,48]{2,1,0:T(4,128)(2,1)S(1)}, u32[]{:S(2)}, u32[]{:S(2)}) collective-permute-start(bf16[20,4,48]{2,1,0:T(4,128)(2,1)S(1)} %get-tuple-element.26), channel_id=1, source_target_pairs={{1,0},{3,2},{5,4},{7,6},{9,8},{11,10},{13,12},{15,14},{17,16},{19,... | collective-permute-start | bytes 23048 | tf_op jit(solution)/shard_map/ppermute | solution.py:18
  46.0 1.8 %collective-permute-done.3 = bf16[20,4,48]{2,1,0:T(4,128)(2,1)S(1)} collective-permute-done((bf16[20,4,48]{2,1,0:T(4,128)(2,1)S(1)}, bf16[20,4,48]{2,1,0:T(4,128)(2,1)S(1)}, u32[]{:S(2)}, u32[]{:S(2)}) %collective-permute-start.3) | collective-permute-done | bytes 7712 | tf_op jit(solution)/shard_map/ppermute | solution.py:18
  47.8 0.1 maximum_maximum_fusion.1
  48.0 0.2 fusion.11
  48.2 0.6 concatenate.20
  48.8 0.0 copy-start.6
  48.8 0.6 copy-done.6
  49.5 0.3 fusion.5
  49.8 2.8 %collective-permute-start.4 = (bf16[8,48,48]{2,1,0:T(8,128)(2,1)S(1)}, bf16[8,48,48]{2,1,0:T(8,128)(2,1)S(1)}, u32[]{:S(2)}, u32[]{:S(2)}) collective-permute-start(bf16[8,48,48]{2,1,0:T(8,128)(2,1)S(1)} %get-tuple-element.29), channel_id=1, source_target_pairs={{0,2},{2,4},{4,6},{6,8},{8,10},{10,12},{12,14},{1,3},{3,5},{5,7},{... | collective-permute-start | bytes 110600 | tf_op jit(solution)/shard_map/ppermute | solution.py:17
  52.7 1.3 %collective-permute-start.5 = (bf16[8,48,48]{2,1,0:T(8,128)(2,1)S(1)}, bf16[8,48,48]{2,1,0:T(8,128)(2,1)S(1)}, u32[]{:S(2)}, u32[]{:S(2)}) collective-permute-start(bf16[8,48,48]{2,1,0:T(8,128)(2,1)S(1)} %get-tuple-element.30), channel_id=1, source_target_pairs={{2,0},{4,2},{6,4},{8,6},{10,8},{12,10},{14,12},{3,1},{5,3},{7,5},{... | collective-permute-start | bytes 110600 | tf_op jit(solution)/shard_map/ppermute | solution.py:18
  54.0 1.1 %collective-permute-done.4 = bf16[8,48,48]{2,1,0:T(8,128)(2,1)S(1)} collective-permute-done((bf16[8,48,48]{2,1,0:T(8,128)(2,1)S(1)}, bf16[8,48,48]{2,1,0:T(8,128)(2,1)S(1)}, u32[]{:S(2)}, u32[]{:S(2)}) %collective-permute-start.4) | collective-permute-done | bytes 36896 | tf_op jit(solution)/shard_map/ppermute | solution.py:17
  55.0 4.2 %collective-permute-done.5 = bf16[8,48,48]{2,1,0:T(8,128)(2,1)S(1)} collective-permute-done((bf16[8,48,48]{2,1,0:T(8,128)(2,1)S(1)}, bf16[8,48,48]{2,1,0:T(8,128)(2,1)S(1)}, u32[]{:S(2)}, u32[]{:S(2)}) %collective-permute-start.5) | collective-permute-done | bytes 36896 | tf_op jit(solution)/shard_map/ppermute | solution.py:18
  59.2 1.3 %collective-permute-start.6 = (bf16[28,8,48]{2,1,0:T(8,128)(2,1)S(1)}, bf16[28,8,48]{2,1,0:T(8,128)(2,1)S(1)}, u32[]{:S(2)}, u32[]{:S(2)}) collective-permute-start(bf16[28,8,48]{2,1,0:T(8,128)(2,1)S(1)} %get-tuple-element.14), channel_id=1, source_target_pairs={{0,1},{2,3},{4,5},{6,7},{8,9},{10,11},{12,13},{14,15},{16,17},{18,... | collective-permute-start | bytes 64520 | tf_op jit(solution)/shard_map/ppermute | solution.py:17
  60.5 1.3 %collective-permute-start.7 = (bf16[28,8,48]{2,1,0:T(8,128)(2,1)S(1)}, bf16[28,8,48]{2,1,0:T(8,128)(2,1)S(1)}, u32[]{:S(2)}, u32[]{:S(2)}) collective-permute-start(bf16[28,8,48]{2,1,0:T(8,128)(2,1)S(1)} %get-tuple-element.15), channel_id=1, source_target_pairs={{1,0},{3,2},{5,4},{7,6},{9,8},{11,10},{13,12},{15,14},{17,16},{19,... | collective-permute-start | bytes 64520 | tf_op jit(solution)/shard_map/ppermute | solution.py:18
  61.8 1.8 %collective-permute-done.7 = bf16[28,8,48]{2,1,0:T(8,128)(2,1)S(1)} collective-permute-done((bf16[28,8,48]{2,1,0:T(8,128)(2,1)S(1)}, bf16[28,8,48]{2,1,0:T(8,128)(2,1)S(1)}, u32[]{:S(2)}, u32[]{:S(2)}) %collective-permute-start.7) | collective-permute-done | bytes 21536 | tf_op jit(solution)/shard_map/ppermute | solution.py:18
  63.6 0.1 maximum_maximum_fusion
  63.8 0.2 fusion.10
  64.0 0.6 concatenate.23
  64.6 0.2 copy-done.2
  64.9 0.4 copy-done.7
  65.3 0.3 fusion.4
  65.6 0.1 reshape.26
  65.7 0.1 copy.22
  65.8 0.8 reshape.35
  66.6 6.0 %all-to-all-start = ((bf16[8,2,1728]{2,1,0:T(2,128)(2,1)}), bf16[8,2,1728]{2,1,0:T(2,128)(2,1)S(1)}, u32[]{:S(2)}, u32[]{:S(2)}) async-start(bf16[8,2,1728]{2,1,0:T(2,128)(2,1)} %reshape.35), calls=%async_computation | async-start | bytes 114688 | tf_op jit(solution)/shard_map/all_to_all | solution.py:100
  72.6 6.8 %all-to-all-done = bf16[8,2,1728]{2,1,0:T(2,128)(2,1)S(1)} async-done(((bf16[8,2,1728]{2,1,0:T(2,128)(2,1)}), bf16[8,2,1728]{2,1,0:T(2,128)(2,1)S(1)}, u32[]{:S(2)}, u32[]{:S(2)}) %all-to-all-start) | async-done | bytes 55328 | tf_op jit(solution)/shard_map/all_to_all | solution.py:100
  79.4 0.2 reshape.36
  79.7 0.2 reshape.37
  79.9 3.8 %all_to_all.10 = bf16[2,2,6912]{2,1,0:T(2,128)(2,1)S(1)} all-to-all(bf16[2,2,6912]{2,1,0:T(2,128)(2,1)S(1)} %reshape.37), channel_id=1, replica_groups=mesh['group'=2,'row'=8,'col'=2] {'col'}, dimensions={0} | all-to-all | bytes 110592 | tf_op jit(solution)/shard_map/all_to_all | solution.py:99
  83.7 0.2 reshape.38
  83.9 0.1 copy.24
  84.0 0.1 constant_dynamic-slice_fusion
  84.1 0.6 collective-permute-start.8
  84.6 6.0 %collective-permute-done.8 = bf16[4,6,12,48]{3,0,2,1:T(4,128)(2,1)S(1)} collective-permute-done((bf16[4,6,12,48]{3,0,2,1:T(4,128)(2,1)S(1)}, bf16[4,6,12,48]{3,0,2,1:T(4,128)(2,1)S(1)}, u32[]{:S(2)}, u32[]{:S(2)}) %collective-permute-start.8) | collective-permute-done | bytes 27680 | tf_op jit(solution)/shard_map/ppermute | solution.py:26
  90.7 0.2 convert_bitcast_fusion
  90.8 0.2 copy.25
  91.1 0.6 copy-done.8
  91.7 0.9 fusion.6
  (27 shorter events, 0.3 us)
Async XLA Ops:
  0.0 48.8 %copy-start = (bf16[3,3,48,48]{3,2,1,0:T(8,128)(2,1)S(1)}, bf16[3,3,48,48]{3,2,1,0:T(8,128)(2,1)}, u32[]{:S(2)}) copy-start(bf16[3,3,48,48]{3,2,1,0:T(8,128)(2,1)} %param.15) | copy-start | bytes 124420
  0.0 0.7 copy-start.5
  0.7 32.3 %copy-start.3 = (bf16[96,48]{0,1:T(8,128)(2,1)S(1)}, bf16[96,48]{0,1:T(8,128)(2,1)}, u32[]{:S(2)}) copy-start(bf16[96,48]{0,1:T(8,128)(2,1)} %param.13) | copy-start | bytes 27652
  0.7 32.5 %copy-start.4 = (bf16[96,48]{0,1:T(8,128)(2,1)S(1)}, bf16[96,48]{0,1:T(8,128)(2,1)}, u32[]{:S(2)}) copy-start(bf16[96,48]{0,1:T(8,128)(2,1)} %param.14) | copy-start | bytes 27652
  33.0 0.9 copy-start.1
  34.0 5.1 %collective-permute-start = (bf16[4,48,48]{2,1,0:T(8,128)(2,1)S(1)}, bf16[4,48,48]{2,1,0:T(8,128)(2,1)S(1)}, u32[]{:S(2)}, u32[]{:S(2)}) collective-permute-start(bf16[4,48,48]{2,1,0:T(8,128)(2,1)S(1)} %get-tuple-element.31), channel_id=1, source_target_pairs={{0,2},{2,4},{4,6},{6,8},{8,10},{10,12},{12,14},{1,3},{3,5},{5,7},{... | collective-permute-start | bytes 55304 | tf_op jit(solution)/shard_map/ppermute | solution.py:17
  37.4 6.0 %collective-permute-start.1 = (bf16[4,48,48]{2,1,0:T(8,128)(2,1)S(1)}, bf16[4,48,48]{2,1,0:T(8,128)(2,1)S(1)}, u32[]{:S(2)}, u32[]{:S(2)}) collective-permute-start(bf16[4,48,48]{2,1,0:T(8,128)(2,1)S(1)} %get-tuple-element.32), channel_id=1, source_target_pairs={{2,0},{4,2},{6,4},{8,6},{10,8},{12,10},{14,12},{3,1},{5,3},{7,5},{... | collective-permute-start | bytes 55304 | tf_op jit(solution)/shard_map/ppermute | solution.py:18
  43.4 2.6 %collective-permute-start.2 = (bf16[20,4,48]{2,1,0:T(4,128)(2,1)S(1)}, bf16[20,4,48]{2,1,0:T(4,128)(2,1)S(1)}, u32[]{:S(2)}, u32[]{:S(2)}) collective-permute-start(bf16[20,4,48]{2,1,0:T(4,128)(2,1)S(1)} %get-tuple-element.25), channel_id=1, source_target_pairs={{0,1},{2,3},{4,5},{6,7},{8,9},{10,11},{12,13},{14,15},{16,17},{18,... | collective-permute-start | bytes 23048 | tf_op jit(solution)/shard_map/ppermute | solution.py:17
  44.7 3.1 %collective-permute-start.3 = (bf16[20,4,48]{2,1,0:T(4,128)(2,1)S(1)}, bf16[20,4,48]{2,1,0:T(4,128)(2,1)S(1)}, u32[]{:S(2)}, u32[]{:S(2)}) collective-permute-start(bf16[20,4,48]{2,1,0:T(4,128)(2,1)S(1)} %get-tuple-element.26), channel_id=1, source_target_pairs={{1,0},{3,2},{5,4},{7,6},{9,8},{11,10},{13,12},{15,14},{17,16},{19,... | collective-permute-start | bytes 23048 | tf_op jit(solution)/shard_map/ppermute | solution.py:18
  48.8 0.7 copy-start.6
  49.8 5.2 %collective-permute-start.4 = (bf16[8,48,48]{2,1,0:T(8,128)(2,1)S(1)}, bf16[8,48,48]{2,1,0:T(8,128)(2,1)S(1)}, u32[]{:S(2)}, u32[]{:S(2)}) collective-permute-start(bf16[8,48,48]{2,1,0:T(8,128)(2,1)S(1)} %get-tuple-element.29), channel_id=1, source_target_pairs={{0,2},{2,4},{4,6},{6,8},{8,10},{10,12},{12,14},{1,3},{3,5},{5,7},{... | collective-permute-start | bytes 110600 | tf_op jit(solution)/shard_map/ppermute | solution.py:17
  52.7 6.5 %collective-permute-start.5 = (bf16[8,48,48]{2,1,0:T(8,128)(2,1)S(1)}, bf16[8,48,48]{2,1,0:T(8,128)(2,1)S(1)}, u32[]{:S(2)}, u32[]{:S(2)}) collective-permute-start(bf16[8,48,48]{2,1,0:T(8,128)(2,1)S(1)} %get-tuple-element.30), channel_id=1, source_target_pairs={{2,0},{4,2},{6,4},{8,6},{10,8},{12,10},{14,12},{3,1},{5,3},{7,5},{... | collective-permute-start | bytes 110600 | tf_op jit(solution)/shard_map/ppermute | solution.py:18
  59.2 2.6 %collective-permute-start.6 = (bf16[28,8,48]{2,1,0:T(8,128)(2,1)S(1)}, bf16[28,8,48]{2,1,0:T(8,128)(2,1)S(1)}, u32[]{:S(2)}, u32[]{:S(2)}) collective-permute-start(bf16[28,8,48]{2,1,0:T(8,128)(2,1)S(1)} %get-tuple-element.14), channel_id=1, source_target_pairs={{0,1},{2,3},{4,5},{6,7},{8,9},{10,11},{12,13},{14,15},{16,17},{18,... | collective-permute-start | bytes 64520 | tf_op jit(solution)/shard_map/ppermute | solution.py:17
  60.5 3.1 %collective-permute-start.7 = (bf16[28,8,48]{2,1,0:T(8,128)(2,1)S(1)}, bf16[28,8,48]{2,1,0:T(8,128)(2,1)S(1)}, u32[]{:S(2)}, u32[]{:S(2)}) collective-permute-start(bf16[28,8,48]{2,1,0:T(8,128)(2,1)S(1)} %get-tuple-element.15), channel_id=1, source_target_pairs={{1,0},{3,2},{5,4},{7,6},{9,8},{11,10},{13,12},{15,14},{17,16},{19,... | collective-permute-start | bytes 64520 | tf_op jit(solution)/shard_map/ppermute | solution.py:18
  64.0 0.9 copy-start.2
  64.6 0.7 copy-start.7
  66.6 12.8 %all-to-all-start = ((bf16[8,2,1728]{2,1,0:T(2,128)(2,1)}), bf16[8,2,1728]{2,1,0:T(2,128)(2,1)S(1)}, u32[]{:S(2)}, u32[]{:S(2)}) async-start(bf16[8,2,1728]{2,1,0:T(2,128)(2,1)} %reshape.35), calls=%async_computation | async-start | bytes 114688 | tf_op jit(solution)/shard_map/all_to_all | solution.py:100
  84.1 6.6 %collective-permute-start.8 = (bf16[4,6,12,48]{3,0,2,1:T(4,128)(2,1)S(1)}, bf16[4,6,12,48]{3,0,2,1:T(4,128)(2,1)S(1)}, u32[]{:S(2)}, u32[]{:S(2)}) collective-permute-start(bf16[4,6,12,48]{3,0,2,1:T(4,128)(2,1)S(1)} %get-tuple-element.28), channel_id=1, source_target_pairs={{0,8},{2,10},{4,12},{6,14},{8,0},{10,2},{12,4},{14,6},{1,9},{3,11}... | collective-permute-start | bytes 82952 | tf_op jit(solution)/shard_map/ppermute | solution.py:26
  91.0 0.7 copy-start.8
  91.0 0.7 copy-start.9
  91.0 0.7 copy-start.10
where the time goes:
time: 93.2 us; the launch traced here: 92.6 us
  blocking collectives  36.1 us (39%)
  waiting for transfers between devices  26.4 us (28%)
  starting transfers between devices  20.5 us (22%)
  local copies, waits for them, and re-layouts  7.02 us (8%)
  matrix products  1.8 us (2%)
    all_gather x1, blocking collectives, on_device(): all_bins = lax.all_gather(embedding, 'row', axis=0, tiled=True)  32.3 us
    ppermute x4, waiting for transfers between devices, padded(): after = lax.ppermute(leading, axis, down)  12 us
    ppermute x4, starting transfers between devices, padded(): before = lax.ppermute(last, axis, up)  8.8 us
    all_to_all x1, waiting for transfers between devices, on_device(): lax.all_to_all(arranged, 'row', split_axis=0, concat_axis=0, tiled=True)  6.85 us
    ppermute x1, waiting for transfers between devices, swapped(): return lax.ppermute(value, axis, pairs)  6.02 us
    all_to_all x1, starting transfers between devices, on_device(): lax.all_to_all(arranged, 'row', split_axis=0, concat_axis=0, tiled=True)  5.98 us
    ppermute x4, starting transfers between devices, padded(): after = lax.ppermute(leading, axis, down)  5.17 us
    unnamed x27, local copies, waits for them, and re-layouts  4.82 us
  transfers between devices with their start and end apart: 10, of which 8 were waited for; matrix products, arithmetic and copies ran while one was open for 0% of the time, Pallas kernels for 0%

commit v1 on v0

--- a/solution.py
+++ b/solution.py
@@ -1,6 +1,10 @@
+import functools
+
 import jax
 import jax.numpy as jnp
 from jax import lax
+from jax.experimental import pallas as pl
+from jax.experimental.pallas import tpu as pltpu
 from jax.sharding import PartitionSpec as P
 
 FIRST_DILATION = 4
@@ -39,6 +43,380 @@
     stacked = jnp.concatenate(windows, axis=-1)
     flat_weight = weight.reshape(9 * weight.shape[2], weight.shape[3])
     return jnp.einsum("rch,hk->rck", stacked, flat_weight, preferred_element_type=jnp.float32)
+
+
+LANES = 128
+HALF = 64
+SIDE = 16
+FUSED_VMEM = 8 * 2**20
+
+
+def one_hot(rows, columns, offsets):
+    r = lax.broadcasted_iota(jnp.int32, (rows, columns), 0)
+    c = lax.broadcasted_iota(jnp.int32, (rows, columns), 1)
+    hit = c == r + offsets[0]
+    for offset in offsets[1:]:
+        hit = hit | (c == r + offset)
+    return jnp.where(hit, 1.0, 0.0)
+
+
+def mm(a, b, precision=None):
+    return jnp.dot(a, b, preferred_element_type=jnp.float32, precision=precision)
+
+
+def fused_kernel(
+    n,
+    m_ref,
+    e_ref,
+    wr_ref,
+    wc_ref,
+    w1_ref,
+    b1_ref,
+    w2_ref,
+    b2_ref,
+    wm_ref,
+    bm_ref,
+    wh_ref,
+    out_ref,
+    pk,
+    eb,
+    ct,
+    rt,
+    xb,
+    rb,
+    pc,
+    l1,
+    rb2,
+    pc2,
+    wa,
+    wb,
+    yb,
+    sb,
+    gb,
+    tb,
+    send,
+    recv,
+    esend,
+    erecv,
+    msend,
+    mrecv,
+    lsem,
+):
+    bf, f32 = jnp.bfloat16, jnp.float32
+    rows, cols, ch = m_ref.shape
+    hr = rows // 2
+    width = cols + SIDE
+    per = cols // rows
+    R = lax.axis_index("row")
+    C = lax.axis_index("col")
+    O = 1 - C
+    group = lax.axis_index("group")
+    mesh_type = pl.DeviceIdType.MESH
+
+    barrier = pltpu.get_barrier_semaphore()
+    for k in range(n):
+        for col in (C, O):
+            if k == 0 and col is C:
+                continue
+            pl.semaphore_signal(
+                barrier, inc=1, device_id=(group, lax.rem(R + k, n), col), device_id_type=mesh_type
+            )
+
+    low = one_hot(ch, LANES, (0,)).astype(bf)
+    high = one_hot(ch, LANES, (HALF,)).astype(bf)
+    both = one_hot(ch, LANES, (0, HALF)).astype(bf)
+    own_at = pl.multiple_of(SIDE * C, SIDE)
+    tile = m_ref[...]
+    packed = mm(tile[:hr].reshape(hr * cols, ch), low) + mm(tile[hr:].reshape(hr * cols, ch), high)
+    pk[1, :, pl.ds(own_at, cols), :] = packed.astype(bf).reshape(hr, cols, LANES)
+    eb[R] = e_ref[...]
+
+    pl.semaphore_wait(barrier, 2 * n - 1)
+
+    def remote(src, dst, s, r, row, col):
+        return pltpu.make_async_remote_copy(
+            src_ref=src,
+            dst_ref=dst,
+            send_sem=s,
+            recv_sem=r,
+            device_id=(group, row, col),
+            device_id_type=mesh_type,
+        )
+
+    embs = []
+    for k in range(1, n):
+        copy = remote(
+            eb.at[R], eb.at[R], esend.at[k - 1], erecv.at[k - 1], lax.rem(R + k, n), C
+        )
+        copy.start()
+        embs.append(copy)
+
+    own_src = pk.at[1, :, pl.ds(own_at, cols), :]
+    side_src = pk.at[1, :, pl.ds(pl.multiple_of(cols - SIDE - (cols - 2 * SIDE) * C, SIDE), SIDE), :]
+    side_at = pl.ds(pl.multiple_of(cols * C, SIDE), SIDE)
+    above = jnp.maximum(R - 1, 0)
+    below = jnp.minimum(R + 1, n - 1)
+    to_below = remote(
+        own_src, pk.at[0, :, pl.ds(own_at, cols), :], send.at[0], recv.at[0], below, C
+    )
+    to_above = remote(
+        own_src, pk.at[2, :, pl.ds(own_at, cols), :], send.at[1], recv.at[1], above, C
+    )
+    to_side = remote(side_src, pk.at[1, :, side_at, :], send.at[2], recv.at[2], R, O)
+    side_below = remote(side_src, pk.at[0, :, side_at, :], send.at[3], recv.at[3], below, O)
+    side_above = remote(side_src, pk.at[2, :, side_at, :], send.at[4], recv.at[4], above, O)
+
+    @pl.when(R < n - 1)
+    def _():
+        to_below.start()
+        side_below.start()
+
+    @pl.when(R > 0)
+    def _():
+        to_above.start()
+        side_above.start()
+
+    to_side.start()
+
+    def pack_weight(w_ref, dst):
+        dst[...] = jnp.zeros_like(dst)
+        taps = ((0, 0), (0, 2), (1, 0), (1, 2), (2, 0), (2, 2), (0, 1), (2, 1), (1, 1))
+        for at, (a, b) in enumerate(taps):
+            dst[at * HALF : at * HALF + ch, :] = mm(w_ref[a, b], both).astype(bf)
+
+    pack_weight(w1_ref, wa)
+    pack_weight(w2_ref, wb)
+    exact = lax.Precision.HIGHEST
+    bias1 = mm(b1_ref[...], both.astype(f32), exact)
+    bias2 = mm(b2_ref[...], both.astype(f32), exact)
+    wr = mm(wr_ref[...], both).astype(bf)
+    wc = mm(wc_ref[...], both).astype(bf)
+    eye = one_hot(ch, ch, (0,))
+    mix_rows = jnp.concatenate([wm_ref[...], jnp.zeros((LANES - ch, ch), bf)], axis=0)
+    nt = (((1,), (1,)), ((), ()))
+    mix_t = lax.dot_general(eye.astype(bf), mix_rows, nt, preferred_element_type=f32).astype(bf)
+    bm = jnp.sum(jnp.where(eye > 0, bm_ref[...], 0.0), axis=1, keepdims=True)
+    wh = jnp.sum(jnp.where(eye > 0, wh_ref[...], 0.0), axis=1, keepdims=True)
+
+    for copy in embs:
+        copy.wait()
+    for k in range(n):
+        block = eb[k]
+        ct[k * rows : (k + 1) * rows, :] = mm(block, wc)
+        rt[k] = mm(block, wr)
+    col_terms = ct[pl.ds(pl.multiple_of((n * rows - width) * C, 8), width), :]
+
+    to_side.wait()
+
+    @pl.when(R > 0)
+    def _():
+        to_below.wait_recv()
+        side_below.wait_recv()
+
+    @pl.when(R < n - 1)
+    def _():
+        to_above.wait_recv()
+        side_above.wait_recv()
+
+    lane = lax.broadcasted_iota(jnp.int32, (1, LANES), 1)
+    lower = lane < HALF
+    col_id = lax.broadcasted_iota(jnp.int32, (width, 1), 0)
+
+    def column_pair(v, d):
+        before = jnp.where(col_id < d, 0.0, pltpu.roll(v, d, axis=0))
+        after = jnp.where(col_id >= width - d, 0.0, pltpu.roll(v, width - d, axis=0))
+        return jnp.where(lower, before, after)
+
+    for b in range(3):
+        at = jnp.clip(R + b - 1, 0, n - 1)
+        terms = rt[at]
+        valid = (R > 0) if b == 0 else (R < n - 1) if b == 2 else None
+        for i in range(hr):
+            v = pk[b, i].astype(f32)
+            turned = pltpu.roll(v, HALF, axis=1)
+            for half, x in ((0, jnp.where(lower, v, turned)), (1, jnp.where(lower, turned, v))):
+                r = i + half * hr
+                x = (x + terms[r : r + 1, :] + col_terms).astype(bf)
+                x = x.astype(f32)
+                if valid is not None:
+                    x = jnp.where(valid, x, 0.0)
+                row = b * rows + r
+                xb[row] = x.astype(bf)
+                x = jnp.maximum(x, 0.0)
+                rb[row] = x.astype(bf)
+                pc[row] = column_pair(x, FIRST_DILATION).astype(bf)
+
+    def conv(p, r, w, first, count, d, at, size):
+        window = pl.ds(at, size)
+
+        def take(ref, shift):
+            return ref[first + shift : first + shift + count, window, :].reshape(
+                count * size, LANES
+            )
+
+        outer = jnp.where(lower, take(r, 0).astype(f32), take(r, 2 * d).astype(f32)).astype(bf)
+        left = jnp.concatenate(
+            [take(p, 0), take(p, d), take(p, 2 * d), outer, take(r, d)], axis=1
+        )
+        return mm(left, w[...]).reshape(count, size, LANES)
+
+    d2 = SECOND_DILATION
+    ext = rows + 2 * d2
+    step = 7 if ext % 7 == 0 else 1
+    for t in range(0, ext, step):
+        acc = conv(pc, rb, wa, t, step, FIRST_DILATION, 0, width)
+        for s in range(step):
+            u = t + s
+            x = (xb[u + FIRST_DILATION].astype(f32) + acc[s] + bias1).astype(bf).astype(f32)
+            if u < d2:
+                x = jnp.where(R > 0, x, 0.0)
+            elif u >= d2 + rows:
+                x = jnp.where(R < n - 1, x, 0.0)
+            else:
+                l1[u - d2] = x.astype(bf)
+            x = jnp.maximum(x, 0.0)
+            rb2[u] = x.astype(bf)
+            pc2[u] = column_pair(x, d2).astype(bf)
+
+    for t in range(0, rows, hr):
+        acc = conv(pc2, rb2, wb, t, hr, d2, own_at, cols)
+        for s in range(hr):
+            base = l1[t + s, pl.ds(own_at, cols), :].astype(f32)
+            yb[t + s] = (base + acc[s] + bias2).astype(bf).astype(f32)
+
+    for i in range(hr):
+        pair = jnp.where(lower, yb[i], yb[i + hr])
+        for j in range(per):
+            sb[j, i] = pair[j * rows : (j + 1) * rows, :].astype(bf)
+
+    mine = lax.rem(R, per)
+    quarter = lax.div(R, per)
+    for j in range(per):
+        peer = per * C + j
+        is_self = (peer == R) & (quarter == C)
+        copy = remote(sb.at[j], gb.at[mine], msend.at[j], mrecv.at[mine], peer, quarter)
+        local = pltpu.make_async_copy(sb.at[j], gb.at[j], lsem)
+
+        @pl.when(jnp.logical_not(is_self))
+        def _():
+            copy.start()
+
+        @pl.when(is_self)
+        def _():
+            local.start()
+
+    for j in range(per):
+        peer = per * C + j
+        is_self = (peer == R) & (quarter == C)
+        arrival = remote(sb.at[j], gb.at[j], msend.at[j], mrecv.at[j], peer, quarter)
+        local = pltpu.make_async_copy(sb.at[j], gb.at[j], lsem)
+
+        @pl.when(jnp.logical_not(is_self))
+        def _():
+            arrival.wait_recv()
+
+        @pl.when(is_self)
+        def _():
+            local.wait()
+
+    pad = tb.shape[0] // cols
+    for j in range(per):
+        for i in range(hr):
+            piece = gb[j, i].astype(f32)
+            at = (j * rows + i) * pad
+            tb[at : at + rows, :] = piece
+            at = (j * rows + i + hr) * pad
+            tb[at : at + rows, :] = pltpu.roll(piece, HALF, axis=1)
+
+    for c in range(rows):
+        mirror = tb[pl.ds(c, cols, stride=pad), :]
+        symmetric = ((yb[c] + mirror) * 0.5).astype(bf)
+        mixed = lax.dot_general(mix_t, symmetric, nt, preferred_element_type=f32) + bm
+        out_ref[c : c + 1, :] = jnp.sum(jnp.maximum(mixed, 0.0) * wh, axis=0, keepdims=True)
+
+    @pl.when(R < n - 1)
+    def _():
+        to_below.wait_send()
+        side_below.wait_send()
+
+    @pl.when(R > 0)
+    def _():
+        to_above.wait_send()
+        side_above.wait_send()
+
+    for j in range(per):
+        peer = per * C + j
+        is_self = (peer == R) & (quarter == C)
+        departure = remote(sb.at[j], gb.at[j], msend.at[j], mrecv.at[j], peer, quarter)
+
+        @pl.when(jnp.logical_not(is_self))
+        def _():
+            departure.wait_send()
+
+
+def fused(map_in, embedding, w_row, w_col, w1, b1, w2, b2, w_mix, b_mix, w_head):
+    rows, cols, ch = map_in.shape
+    n = lax.axis_size("row")
+    width, ext, per, hr = cols + SIDE, rows + 2 * SECOND_DILATION, cols // rows, rows // 2
+    bf, f32 = jnp.bfloat16, jnp.float32
+    dma = pltpu.SemaphoreType.DMA
+    return pl.pallas_call(
+        functools.partial(fused_kernel, n),
+        out_shape=jax.ShapeDtypeStruct((rows, cols), f32),
+        in_specs=[pl.BlockSpec(memory_space=pltpu.VMEM)] * 11,
+        out_specs=pl.BlockSpec(memory_space=pltpu.VMEM),
+        scratch_shapes=[
+            pltpu.VMEM((3, hr, width, LANES), bf),
+            pltpu.VMEM((n, rows, embedding.shape[1]), bf),
+            pltpu.VMEM((n * rows, LANES), f32),
+            pltpu.VMEM((n, rows, LANES), f32),
+            pltpu.VMEM((3 * rows, width, LANES), bf),
+            pltpu.VMEM((3 * rows, width, LANES), bf),
+            pltpu.VMEM((3 * rows, width, LANES), bf),
+            pltpu.VMEM((rows, width, LANES), bf),
+            pltpu.VMEM((ext, width, LANES), bf),
+            pltpu.VMEM((ext, width, LANES), bf),
+            pltpu.VMEM((10 * HALF, LANES), bf),
+            pltpu.VMEM((10 * HALF, LANES), bf),
+            pltpu.VMEM((rows, cols, LANES), f32),
+            pltpu.VMEM((per, hr, rows, LANES), bf),
+            pltpu.VMEM((per, hr, rows, LANES), bf),
+            pltpu.VMEM((cols * 16, LANES), f32),
+            dma((5,)),
+            dma((5,)),
+            dma((n - 1,)),
+            dma((n - 1,)),
+            dma((per,)),
+            dma((per,)),
+            dma,
+        ],
+        compiler_params=pltpu.CompilerParams(collective_id=0, has_side_effects=True),
+    )(
+        map_in,
+        embedding,
+        w_row,
+        w_col,
+        w1,
+        b1.reshape(1, ch),
+        w2,
+        b2.reshape(1, ch),
+        w_mix,
+        b_mix.reshape(1, ch),
+        w_head.reshape(1, ch),
+    )
+
+
+def fits(rows, cols, channels, row_count, col_count):
+    scratch = 2 * LANES * (cols + SIDE) * (16 * rows + 6 * SECOND_DILATION)
+    halo = FIRST_DILATION + SECOND_DILATION
+    return (
+        scratch <= FUSED_VMEM
+        and rows == halo
+        and col_count == 2
+        and cols % SIDE == 0
+        and channels <= 48
+        and cols * col_count == rows * row_count
+    )
 
 
 def on_device(
@@ -56,6 +434,20 @@
 ):
     patch_rows, patch_columns, channels = map_in.shape
     row_count = lax.axis_size("row")
+    if fits(patch_rows, patch_columns, channels, row_count, lax.axis_size("col")):
+        return fused(
+            map_in,
+            embedding,
+            w_row,
+            w_col,
+            first_kernel_weight,
+            first_bias,
+            second_kernel_weight,
+            second_bias,
+            w_mix,
+            b_mix,
+            w_head,
+        )
     row_at = lax.axis_index("row")
     col_at = lax.axis_index("col")
     all_bins = lax.all_gather(embedding, "row", axis=0, tiled=True)

time: 93.2 us -> 22.9 us (0.25)
  blocking collectives: 36.1 us -> 0 us
  waiting for transfers between devices: 26.4 us -> 0 us
  starting transfers between devices: 20.5 us -> 0 us
  Pallas kernels: 0 us -> 19.1 us
  local copies, waits for them, and re-layouts: 7.02 us -> 3.43 us
  matrix products: 1.8 us -> 0 us
    all_gather x1 -> x0, blocking collectives: 32.3 us -> none  [on_device(): all_bins = lax.all_gather(embedding, 'row', axis=0, tiled=True)]
    ppermute x9 -> x0, waiting for transfers between devices: 19.5 us -> none  [the longest x4 12 us: padded(): after = lax.ppermute(leading, axis, down)]
    pallas_call x0 -> x1, Pallas kernels: none -> 19.1 us  [fused(): pl.pallas_call(functools.partial(fused_kernel, n), out_shape=jax.ShapeDty...]
    ppermute x9 -> x0, starting transfers between devices: 14.5 us -> none  [the longest x4 8.8 us: padded(): before = lax.ppermute(last, axis, up)]
    all_to_all x1 -> x0, waiting for transfers between devices: 6.85 us -> none  [on_device(): lax.all_to_all(arranged, 'row', split_axis=0, concat_axis=0, tiled=True)]
    all_to_all x1 -> x0, starting transfers between devices: 5.98 us -> none  [on_device(): lax.all_to_all(arranged, 'row', split_axis=0, concat_axis=0, tiled=True)]
    all_to_all x1 -> x0, blocking collectives: 3.77 us -> none  [on_device(): lax.all_to_all(lax.all_to_all(arranged, 'row', split_axis=0, concat_axis=...]
    dot_general x5 -> x0, matrix products: 1.8 us -> none  [the longest x1 0.92 us: on_device(): jnp.einsum('rch,hk->rck', symmetric, w_mix, preferred_element_type=jnp.fl...]
  transfers between devices with their start and end apart: 10 -> 0, of which waited for: 8 -> 0; matrix products, arithmetic and copies ran while one was open for 0% -> 0% of each run, Pallas kernels for 0% -> 0%
where the time goes in v1:
time: 22.9 us; the launch traced here: 22.6 us
  Pallas kernels  19.1 us (83%)
  local copies, waits for them, and re-layouts  3.43 us (15%)
    pallas_call x1, Pallas kernels, fused(): pl.pallas_call(functools.partial(fused_kernel, n), out_shape=jax.ShapeDty...  19.1 us
    unnamed x5, local copies, waits for them, and re-layouts  3.43 us

profile of v1, /device:TPU:0, one launch (start us, length us, event | category | flops | bytes accessed | tf_op | source)
XLA Modules:
  0.0 22.6 jit_solution(8624305894743640635)
XLA Ops:
  0.0 0.0 copy-start
  0.0 1.4 %copy.12.wr_ref = bf16[96,48]{1,0:T(8,128)(2,1)} copy(bf16[96,48]{0,1:T(8,128)(2,1)} %param.13) | data formatting | bytes 18432 | tf_op args[2]
  1.4 0.0 copy-done
  1.4 0.7 %copy.13.wc_ref = bf16[96,48]{1,0:T(8,128)(2,1)} copy(bf16[96,48]{0,1:T(8,128)(2,1)S(1)} %copy-done) | data formatting | bytes 18432 | tf_op args[3]
  2.1 19.1 %shard_map.109 = f32[12,48]{1,0:T(8,128)} custom-call(bf16[12,48,48]{2,1,0:T(8,128)(2,1)} %m_ref.1, bf16[12,96]{1,0:T(8,128)(2,1)} %e_ref.1, bf16[96,48]{1,0:T(8,128)(2,1)} %copy.12.wr_ref, bf16[96,48]{1,0:T(8,128)(2,1)} %copy.13.wc_ref, bf16[3,3,48,48]{3,2,1,0:T(8,128)(2,1)} %w1_ref.1, f32[1,48]{1,0:T(1,128)} %bitcast.4, bf16[3,3,48,48]{3,2,1,0:T(8,128)(2,1)} %w2_ref.1, ...), custom_call_target="tpu_custom_call" | custom-call | tf_op jit(solution)/shard_map/pallas_call | solution.py:363
  21.3 1.3 %copy.15 = f32[12,48]{1,0:T(8,128)} copy(f32[12,48]{1,0:T(8,128)} %shard_map.109) | data formatting | bytes 4608
Async XLA Ops:
  0.0 1.4 %copy-start = (bf16[96,48]{0,1:T(8,128)(2,1)S(1)}, bf16[96,48]{0,1:T(8,128)(2,1)}, u32[]{:S(2)}) copy-start(bf16[96,48]{0,1:T(8,128)(2,1)} %param.14) | copy-start | bytes 27652

commit v2 on v1

--- a/solution.py
+++ b/solution.py
@@ -62,6 +62,10 @@
 
 def mm(a, b, precision=None):
     return jnp.dot(a, b, preferred_element_type=jnp.float32, precision=precision)
+
+
+def mm_nt(a, b):
+    return lax.dot_general(a, b, (((1,), (1,)), ((), ())), preferred_element_type=jnp.float32)
 
 
 def fused_kernel(
@@ -189,12 +193,12 @@
     exact = lax.Precision.HIGHEST
     bias1 = mm(b1_ref[...], both.astype(f32), exact)
     bias2 = mm(b2_ref[...], both.astype(f32), exact)
-    wr = mm(wr_ref[...], both).astype(bf)
-    wc = mm(wc_ref[...], both).astype(bf)
+    gap = jnp.zeros((HALF - ch, wr_ref.shape[1]), bf)
+    wr = jnp.concatenate([wr_ref[...], gap, wr_ref[...], gap], axis=0)
+    wc = jnp.concatenate([wc_ref[...], gap, wc_ref[...], gap], axis=0)
     eye = one_hot(ch, ch, (0,))
     mix_rows = jnp.concatenate([wm_ref[...], jnp.zeros((LANES - ch, ch), bf)], axis=0)
-    nt = (((1,), (1,)), ((), ()))
-    mix_t = lax.dot_general(eye.astype(bf), mix_rows, nt, preferred_element_type=f32).astype(bf)
+    mix_t = mm_nt(eye.astype(bf), mix_rows).astype(bf)
     bm = jnp.sum(jnp.where(eye > 0, bm_ref[...], 0.0), axis=1, keepdims=True)
     wh = jnp.sum(jnp.where(eye > 0, wh_ref[...], 0.0), axis=1, keepdims=True)
 
@@ -202,8 +206,8 @@
         copy.wait()
     for k in range(n):
         block = eb[k]
-        ct[k * rows : (k + 1) * rows, :] = mm(block, wc)
-        rt[k] = mm(block, wr)
+        ct[k * rows : (k + 1) * rows, :] = mm_nt(block, wc)
+        rt[k] = mm_nt(block, wr)
     col_terms = ct[pl.ds(pl.multiple_of((n * rows - width) * C, 8), width), :]
 
     to_side.wait()
@@ -331,7 +335,7 @@
     for c in range(rows):
         mirror = tb[pl.ds(c, cols, stride=pad), :]
         symmetric = ((yb[c] + mirror) * 0.5).astype(bf)
-        mixed = lax.dot_general(mix_t, symmetric, nt, preferred_element_type=f32) + bm
+        mixed = mm_nt(mix_t, symmetric) + bm
         out_ref[c : c + 1, :] = jnp.sum(jnp.maximum(mixed, 0.0) * wh, axis=0, keepdims=True)
 
     @pl.when(R < n - 1)
@@ -394,8 +398,8 @@
     )(
         map_in,
         embedding,
-        w_row,
-        w_col,
+        w_row.T,
+        w_col.T,
         w1,
         b1.reshape(1, ch),
         w2,

time: 22.9 us -> 20.7 us (0.904)
  local copies, waits for them, and re-layouts: 3.43 us -> 1.3 us
    unnamed x5 -> x1, local copies, waits for them, and re-layouts: 3.43 us -> 1.3 us
where the time goes in v2:
time: 20.7 us; the launch traced here: 20.5 us
  Pallas kernels  19.2 us (93%)
  local copies, waits for them, and re-layouts  1.3 us (6%)
    pallas_call x1, Pallas kernels, fused(): pl.pallas_call(functools.partial(fused_kernel, n), out_shape=jax.ShapeDty...  19.2 us
    unnamed x1, local copies, waits for them, and re-layouts  1.3 us

profile of v2, /device:TPU:0, one launch (start us, length us, event | category | flops | bytes accessed | tf_op | source)
XLA Modules:
  0.0 20.5 jit_solution(14453084946965070831)
XLA Ops:
  0.0 19.2 %shard_map.109 = f32[12,48]{1,0:T(8,128)} custom-call(bf16[12,48,48]{2,1,0:T(8,128)(2,1)} %m_ref.1, bf16[12,96]{1,0:T(8,128)(2,1)} %e_ref.1, bf16[48,96]{1,0:T(8,128)(2,1)} %bitcast.6, bf16[48,96]{1,0:T(8,128)(2,1)} %bitcast.7, bf16[3,3,48,48]{3,2,1,0:T(8,128)(2,1)} %w1_ref.1, f32[1,48]{1,0:T(1,128)} %bitcast.8, bf16[3,3,48,48]{3,2,1,0:T(8,128)(2,1)} %w2_ref.1, ...), custom_call_target="tpu_custom_call" | custom-call | tf_op jit(solution)/shard_map/pallas_call | solution.py:367
  19.2 1.3 %copy.13 = f32[12,48]{1,0:T(8,128)} copy(f32[12,48]{1,0:T(8,128)} %shard_map.109) | data formatting | bytes 4608

commit v3 on v2

--- a/solution.py
+++ b/solution.py
@@ -366,7 +366,7 @@
     dma = pltpu.SemaphoreType.DMA
     return pl.pallas_call(
         functools.partial(fused_kernel, n),
-        out_shape=jax.ShapeDtypeStruct((rows, cols), f32),
+        out_shape=pltpu.VMEM((rows, cols), f32),
         in_specs=[pl.BlockSpec(memory_space=pltpu.VMEM)] * 11,
         out_specs=pl.BlockSpec(memory_space=pltpu.VMEM),
         scratch_shapes=[

time: 20.7 us -> 19.3 us (0.932)
  local copies, waits for them, and re-layouts: 1.3 us -> 0.6 us
  Pallas kernels: 19.2 us -> 18.6 us
    unnamed x1, local copies, waits for them, and re-layouts: 1.3 us -> 0.6 us
    pallas_call x1, Pallas kernels: 19.2 us -> 18.6 us  [fused(): pl.pallas_call(functools.partial(fused_kernel, n), out_shape=pltpu.VMEM((...]
where the time goes in v3:
time: 19.3 us; the launch traced here: 19.2 us
  Pallas kernels  18.6 us (96%)
  local copies, waits for them, and re-layouts  0.6 us (3%)
    pallas_call x1, Pallas kernels, fused(): pl.pallas_call(functools.partial(fused_kernel, n), out_shape=pltpu.VMEM((...  18.6 us
    unnamed x1, local copies, waits for them, and re-layouts  0.6 us

profile of v3, /device:TPU:0, one launch (start us, length us, event | category | flops | bytes accessed | tf_op | source)
XLA Modules:
  0.0 19.2 jit_solution(9025478584579008266)
XLA Ops:
  0.0 18.6 %shard_map.109 = f32[12,48]{1,0:T(8,128)S(1)} custom-call(bf16[12,48,48]{2,1,0:T(8,128)(2,1)} %m_ref.1, bf16[12,96]{1,0:T(8,128)(2,1)} %e_ref.1, bf16[48,96]{1,0:T(8,128)(2,1)} %bitcast.6, bf16[48,96]{1,0:T(8,128)(2,1)} %bitcast.7, bf16[3,3,48,48]{3,2,1,0:T(8,128)(2,1)} %w1_ref.1, f32[1,48]{1,0:T(1,128)} %bitcast.8, bf16[3,3,48,48]{3,2,1,0:T(8,128)(2,1)} %w2_ref.1, ...), custom_call_target="tpu_custom_call" | custom-call | tf_op jit(solution)/shard_map/pallas_call | solution.py:367
  18.6 0.6 %copy.13 = f32[12,48]{1,0:T(8,128)} copy(f32[12,48]{1,0:T(8,128)S(1)} %shard_map.109) | data formatting | bytes 4608

commit v4 on v3

--- a/solution.py
+++ b/solution.py
@@ -70,17 +70,17 @@
 
 def fused_kernel(
     n,
-    m_ref,
-    e_ref,
-    wr_ref,
-    wc_ref,
-    w1_ref,
-    b1_ref,
-    w2_ref,
-    b2_ref,
-    wm_ref,
-    bm_ref,
-    wh_ref,
+    m_hbm,
+    e_hbm,
+    wr_hbm,
+    wc_hbm,
+    w1_hbm,
+    b1_hbm,
+    w2_hbm,
+    b2_hbm,
+    wm_hbm,
+    bm_hbm,
+    wh_hbm,
     out_ref,
     pk,
     eb,
@@ -105,6 +105,18 @@
     msend,
     mrecv,
     lsem,
+    isem,
+    m_ref,
+    e_ref,
+    wr_ref,
+    wc_ref,
+    w1_ref,
+    b1_ref,
+    w2_ref,
+    b2_ref,
+    wm_ref,
+    bm_ref,
+    wh_ref,
 ):
     bf, f32 = jnp.bfloat16, jnp.float32
     rows, cols, ch = m_ref.shape
@@ -126,13 +138,32 @@
                 barrier, inc=1, device_id=(group, lax.rem(R + k, n), col), device_id_type=mesh_type
             )
 
+    inputs = (
+        (m_hbm, m_ref),
+        (e_hbm, e_ref),
+        (wr_hbm, wr_ref),
+        (wc_hbm, wc_ref),
+        (w1_hbm, w1_ref),
+        (b1_hbm, b1_ref),
+        (w2_hbm, w2_ref),
+        (b2_hbm, b2_ref),
+        (wm_hbm, wm_ref),
+        (bm_hbm, bm_ref),
+        (wh_hbm, wh_ref),
+    )
+    loads = [pltpu.make_async_copy(a, b, isem.at[i]) for i, (a, b) in enumerate(inputs)]
+    for load in loads:
+        load.start()
+
     low = one_hot(ch, LANES, (0,)).astype(bf)
     high = one_hot(ch, LANES, (HALF,)).astype(bf)
     both = one_hot(ch, LANES, (0, HALF)).astype(bf)
     own_at = pl.multiple_of(SIDE * C, SIDE)
+    loads[0].wait()
     tile = m_ref[...]
     packed = mm(tile[:hr].reshape(hr * cols, ch), low) + mm(tile[hr:].reshape(hr * cols, ch), high)
     pk[1, :, pl.ds(own_at, cols), :] = packed.astype(bf).reshape(hr, cols, LANES)
+    loads[1].wait()
     eb[R] = e_ref[...]
 
     pl.semaphore_wait(barrier, 2 * n - 1)
@@ -188,6 +219,8 @@
         for at, (a, b) in enumerate(taps):
             dst[at * HALF : at * HALF + ch, :] = mm(w_ref[a, b], both).astype(bf)
 
+    for load in loads[2:]:
+        load.wait()
     pack_weight(w1_ref, wa)
     pack_weight(w2_ref, wb)
     exact = lax.Precision.HIGHEST
@@ -364,10 +397,23 @@
     width, ext, per, hr = cols + SIDE, rows + 2 * SECOND_DILATION, cols // rows, rows // 2
     bf, f32 = jnp.bfloat16, jnp.float32
     dma = pltpu.SemaphoreType.DMA
+    operands = (
+        map_in,
+        embedding,
+        w_row.T,
+        w_col.T,
+        w1,
+        b1.reshape(1, ch),
+        w2,
+        b2.reshape(1, ch),
+        w_mix,
+        b_mix.reshape(1, ch),
+        w_head.reshape(1, ch),
+    )
     return pl.pallas_call(
         functools.partial(fused_kernel, n),
         out_shape=pltpu.VMEM((rows, cols), f32),
-        in_specs=[pl.BlockSpec(memory_space=pltpu.VMEM)] * 11,
+        in_specs=[pl.BlockSpec(memory_space=pl.ANY)] * 11,
         out_specs=pl.BlockSpec(memory_space=pltpu.VMEM),
         scratch_shapes=[
             pltpu.VMEM((3, hr, width, LANES), bf),
@@ -393,21 +439,11 @@
             dma((per,)),
             dma((per,)),
             dma,
+            dma((11,)),
+            *[pltpu.VMEM(x.shape, x.dtype) for x in operands],
         ],
         compiler_params=pltpu.CompilerParams(collective_id=0, has_side_effects=True),
-    )(
-        map_in,
-        embedding,
-        w_row.T,
-        w_col.T,
-        w1,
-        b1.reshape(1, ch),
-        w2,
-        b2.reshape(1, ch),
-        w_mix,
-        b_mix.reshape(1, ch),
-        w_head.reshape(1, ch),
-    )
+    )(*operands)
 
 
 def fits(rows, cols, channels, row_count, col_count):

time: 19.3 us -> 18.3 us (0.948)
  Pallas kernels: 18.6 us -> 17.6 us
    pallas_call x1, Pallas kernels: 18.6 us -> 17.6 us  [fused(): pl.pallas_call(functools.partial(fused_kernel, n), out_shape=pltpu.VMEM((...]
where the time goes in v4:
time: 18.3 us; the launch traced here: 18.2 us
  Pallas kernels  17.6 us (96%)
  local copies, waits for them, and re-layouts  0.6 us (3%)
    pallas_call x1, Pallas kernels, fused(): pl.pallas_call(functools.partial(fused_kernel, n), out_shape=pltpu.VMEM((...  17.6 us
    unnamed x1, local copies, waits for them, and re-layouts  0.6 us

profile of v4, /device:TPU:0, one launch (start us, length us, event | category | flops | bytes accessed | tf_op | source)
XLA Modules:
  0.0 18.2 jit_solution(10196997978182631221)
XLA Ops:
  0.0 17.6 %shard_map.109 = f32[12,48]{1,0:T(8,128)S(1)} custom-call(bf16[12,48,48]{2,1,0:T(8,128)(2,1)} %m_hbm.1, bf16[12,96]{1,0:T(8,128)(2,1)} %e_hbm.1, bf16[48,96]{1,0:T(8,128)(2,1)} %bitcast.6, bf16[48,96]{1,0:T(8,128)(2,1)} %bitcast.7, bf16[3,3,48,48]{3,2,1,0:T(8,128)(2,1)} %w1_hbm.1, f32[1,48]{1,0:T(1,128)} %bitcast.8, bf16[3,3,48,48]{3,2,1,0:T(8,128)(2,1)} %w2_hbm.1, ...), custom_call_target="tpu_custom_call" | custom-call | tf_op jit(solution)/shard_map/pallas_call | solution.py:413
  17.6 0.6 %copy.13 = f32[12,48]{1,0:T(8,128)} copy(f32[12,48]{1,0:T(8,128)S(1)} %shard_map.109) | data formatting | bytes 4608
